TPU v7x, 256 devices: a whole 4x4x8 slice. The times are simulated.
256 devices in a mesh: gx: 4 (over y), gy: 4 (over x), gz: 16 (over z, core).
Axes of the slice: x: 4, y: 4, z: 8, core: 2. Of those that a mesh axis runs over, the one named last changes fastest.
Arguments:
- rhs: float32 [4, 4, 16, 64, 1536], P('gx', 'gy', 'gz'), may hold values from -20 to 20
- dual_block: bfloat16 [4, 4, 16, 1536, 1536], P('gx', 'gy', 'gz'), may hold values from -1 to 4, as said below
- schur_block: bfloat16 [4, 4, 16, 1536, 1536], P('gx', 'gy', 'gz'), may hold values from -1 to 2, as said below
- dual_scale: float32 [4, 4, 16, 1536], P('gx', 'gy', 'gz'), may hold values from 0.5 to 1.5
- dof_order: int32 [4, 4, 16, 1536], P('gx', 'gy', 'gz'), may hold values from 0 to 1535, each once within a row
- modes: float32 [4, 4, 16, 1536, 24], P('gx', 'gy', 'gz'), may hold values from -0.21875 to 0.21875
- coarse_inverse: float32 [6144, 6144], P(('gx', 'gy', 'gz')), may hold values from -1 to 4, as said below
- step_scale: float32 [2], replicated, may hold values from 0.5 to 1
Outputs:
- multipliers: float32 [4, 4, 16, 64, 1536], P('gx', 'gy', 'gz')
- residual: float32 [4, 4, 16, 64, 1536], P('gx', 'gy', 'gz')
Inputs may be any that keep to these rules, and one draw needn't show every extreme that they name: For each subdomain, dof_order is a permutation of 0 to 1535. `dual_block`: Symmetric. `schur_block`: Symmetric. `coarse_inverse`: Symmetric.
All inputs are finite; a program needn't handle non-finite values.
Results may differ from a plain program's by a relative error of at most 0.0045.
Values sent between devices are 32-bit elements; how exact they have to be, the bound alone decides.
No kernel may reach another device: no remote copies, remote signals or barrier semaphores. Data moves between devices by JAX's collectives and lax.ppermute only.
A program may use at most 128 MiB of HBM per device.

v0:
```python
import jax
import jax.numpy as jnp
from jax import lax
from jax.sharding import PartitionSpec as P

ITERS = 2
HIGH = lax.Precision.HIGHEST


def extended(cells, sides, width):
    for axis, dim in sides:
        count = lax.axis_size(axis)
        ends = count - 1
        head = lax.slice_in_dim(cells, 0, width, axis=dim)
        tail = lax.slice_in_dim(cells, cells.shape[dim] - width, cells.shape[dim], axis=dim)
        cells = jnp.concatenate(
            [
                lax.ppermute(tail, axis, [(i, (i + 1) % count) for i in range(ends)]),
                cells,
                lax.ppermute(head, axis, [((i + 1) % count, i) for i in range(ends)]),
            ],
            axis=dim,
        )
    return cells


def reorder(matrix, order):
    rows = jnp.take(matrix, order, axis=0)
    return jnp.take(rows, order, axis=1)


def assemble(field):
    loads, width = field.shape
    faces = field.reshape(loads, 6, width // 6)
    ext_x = extended(jnp.stack([faces[:, 0], faces[:, 1]]), (("gx", 0),), 1)
    ext_y = extended(jnp.stack([faces[:, 2], faces[:, 3]]), (("gy", 0),), 1)
    ext_z = extended(jnp.stack([faces[:, 4], faces[:, 5]]), (("gz", 0),), 1)
    parts = [
        faces[:, 0] + ext_x[0],
        faces[:, 1] + ext_x[3],
        faces[:, 2] + ext_y[0],
        faces[:, 3] + ext_y[3],
        faces[:, 4] + ext_z[0],
        faces[:, 5] + ext_z[3],
    ]
    return jnp.stack(parts, axis=1).reshape(loads, width)


def project(field, basis, coarse_rows):
    weights = jnp.dot(field, basis, precision=HIGH)
    share = jnp.dot(
        lax.all_gather(weights, ("gx", "gy", "gz"), axis=1, tiled=True),
        coarse_rows.T,
        precision=HIGH,
    )
    correction = jnp.dot(share, basis.T, precision=HIGH)
    return field - assemble(correction)


def shards(rhs, dual_block, schur_block, dual_scale, dof_order, modes, coarse_inverse, step_scale):
    residual = rhs[0, 0, 0]
    order = dof_order[0, 0, 0]
    dual = reorder(dual_block[0, 0, 0], order)
    schur = reorder(schur_block[0, 0, 0], order)
    scale = dual_scale[0, 0, 0]
    basis = modes[0, 0, 0]

    def precondition(field):
        applied = jnp.dot(field.astype(jnp.bfloat16), schur, preferred_element_type=jnp.float32)
        return project(assemble(applied), basis, coarse_inverse)

    multipliers = jnp.zeros_like(residual)
    search = precondition(residual)
    for iteration in range(ITERS):
        image = scale * jnp.dot(
            (scale * search).astype(jnp.bfloat16), dual, preferred_element_type=jnp.float32
        )
        image = project(assemble(image), basis, coarse_inverse)
        later = iteration + 1 < ITERS
        along, energy = lax.psum(
            (jnp.sum(residual * image, axis=1), jnp.sum(image * image, axis=1)), ("gx", "gy", "gz")
        )
        alpha = step_scale[iteration] * along / (energy + 1e-06)
        multipliers = multipliers + alpha[:, None] * search
        residual = residual - alpha[:, None] * image
        if later:
            search = precondition(residual)
    return (multipliers[None, None, None], residual[None, None, None])


def solution(mesh):
    in_specs = (
        P("gx", "gy", "gz", None, None),
        P("gx", "gy", "gz", None, None),
        P("gx", "gy", "gz", None, None),
        P("gx", "gy", "gz", None),
        P("gx", "gy", "gz", None),
        P("gx", "gy", "gz", None, None),
        P(("gx", "gy", "gz"), None),
        P(),
    )
    out_specs = (P("gx", "gy", "gz", None, None), P("gx", "gy", "gz", None, None))
    return jax.shard_map(shards, mesh=mesh, in_specs=in_specs, out_specs=out_specs, check_vma=False)
```

profile of v0, /device:TPU:1, one launch (start us, length us, event | category | flops | bytes accessed | tf_op | source)
XLA Modules:
  0.0 909.4 jit_solution(9672217971376196631)
XLA Ops:
  8.0 13.3 %gather_fusion.2 = bf16[1536,1536]{1,0:T(8,128)(2,1)} fusion(bf16[1536,1536]{1,0:T(8,128)(2,1)} %bitcast.399, s32[2048]{0:T(1024)S(1)} %pad_clamp_fusion), kind=kCustom, calls=%fused_computation.2.clone | custom fusion | bytes 9443328 | tf_op jit(solution)/shard_map/jit(_take)/gather | solution.py:28
  21.4 13.3 %gather_fusion = bf16[1536,1536]{1,0:T(8,128)(2,1)} fusion(bf16[1536,1536]{1,0:T(8,128)(2,1)} %bitcast.400, s32[2048]{0:T(1024)S(1)} %pad_clamp_fusion), kind=kCustom, calls=%fused_computation.clone | custom fusion | bytes 9443328 | tf_op jit(solution)/shard_map/jit(_take)/gather | solution.py:28
  34.7 8.7 broadcast_select_fusion
  43.4 6.7 copy.72
  50.0 13.3 %gather_fusion.1 = bf16[1536,1536]{1,0:T(8,128)(2,1)} fusion(bf16[1536,1536]{0,1:T(8,128)(2,1)} %copy.72, s32[2048]{0:T(1024)S(1)} %pad_clamp_fusion), kind=kCustom, calls=%fused_computation.1.clone | custom fusion | bytes 9443328 | tf_op jit(solution)/shard_map/jit(_take)/gather | solution.py:29
  63.4 2.9 broadcast_select_fusion.3
  66.3 2.2 copy-done.1
  68.4 1.5 fusion.12
  70.4 4.0 collective-permute-start
  77.1 3.1 collective-permute-start.2
  82.8 5.8 collective-permute-start.4
  90.0 2.4 collective-permute-start.5
  92.4 3.8 collective-permute-done.5
  98.3 111.7 %all-gather.5.cloned.1.call-done = f32[64,6144]{0,1:T(8,128)} async-done(((f32[64,24]{0,1:T(8,128)}), f32[64,6144]{0,1:T(8,128)}) %all-gather.5.cloned.1.call-update) | async-done | bytes 1572880 | tf_op jit(solution)/shard_map/all_gather | solution.py:52
  210.1 3.7 convolution_bitcast_fusion.3
  214.4 3.0 collective-permute-start.6
  217.4 6.6 copy.82
  224.0 13.3 %gather_fusion.3 = bf16[1536,1536]{1,0:T(8,128)(2,1)} fusion(bf16[1536,1536]{0,1:T(8,128)(2,1)} %copy.82, s32[2048]{0:T(1024)S(1)} %pad_clamp_fusion), kind=kCustom, calls=%fused_computation.3.clone | custom fusion | bytes 9443328 | tf_op jit(solution)/shard_map/jit(_take)/gather | solution.py:29
  237.4 2.4 collective-permute-start.11
  242.5 3.1 collective-permute-start.10
  245.6 4.3 collective-permute-start.8
  251.4 3.8 fusion.6
  255.6 4.2 collective-permute-start.12
  259.8 1.8 collective-permute-done.12
  263.0 3.4 collective-permute-start.14
  269.2 4.6 collective-permute-start.16
  275.1 2.7 collective-permute-start.17
  277.8 3.5 collective-permute-done.17
  282.4 109.9 %all-gather.7.cloned.1.call-done = f32[64,6144]{0,1:T(8,128)} async-done(((f32[64,24]{0,1:T(8,128)}), f32[64,6144]{0,1:T(8,128)}) %all-gather.7.cloned.1.call-update) | async-done | bytes 1572880 | tf_op jit(solution)/shard_map/all_gather | solution.py:52
  392.3 3.7 convolution_bitcast_fusion.2
  396.6 3.0 collective-permute-start.18
  400.3 2.4 collective-permute-start.23
  405.3 3.1 collective-permute-start.22
  408.4 4.3 collective-permute-start.20
  415.7 79.7 %all-reduce.1 = (f32[64]{0:T(128)S(1)}, f32[64]{0:T(128)S(1)}) all-reduce(f32[64]{0:T(128)S(1)} %get-tuple-element.12, f32[64]{0:T(128)S(1)} %get-tuple-element.10), channel_id=1, replica_groups=mesh['gx'=4,'gy'=4,'gz'=16] {'gx','gy','gz'}, use_global_device_ids=true, to_apply=%region_3.6 | all-reduce | flops 128 | bytes 1024 | tf_op jit(solution)/shard_map/psum | solution.py:80
  496.0 3.9 fusion.18
  501.2 2.9 collective-permute-start.29
  506.7 2.7 collective-permute-start.28
  509.4 4.3 collective-permute-start.26
  513.8 1.8 collective-permute-done.26
  516.9 106.0 %all-gather.9.cloned.1.call-done = f32[64,6144]{0,1:T(8,128)} async-done(((f32[64,24]{0,1:T(8,128)}), f32[64,6144]{0,1:T(8,128)}) %all-gather.9.cloned.1.call-update) | async-done | bytes 1572880 | tf_op jit(solution)/shard_map/all_gather | solution.py:52
  622.9 3.7 convolution_bitcast_fusion.1
  627.1 3.0 collective-permute-start.30
  630.2 2.4 collective-permute-start.35
  635.2 3.1 collective-permute-start.34
  638.4 4.3 collective-permute-start.32
  644.2 4.8 fusion.9
  649.0 1.9 reshape.280
  651.0 2.8 fusion.42
  653.7 4.2 collective-permute-start.36
  658.0 1.8 collective-permute-done.36
  661.1 3.4 collective-permute-start.38
  664.5 1.4 collective-permute-done.37
  667.3 4.6 collective-permute-start.40
  673.2 2.7 collective-permute-start.41
  675.9 3.5 collective-permute-done.41
  680.5 110.0 %all-gather.11.cloned.1.call-done = f32[64,6144]{0,1:T(8,128)} async-done(((f32[64,24]{0,1:T(8,128)}), f32[64,6144]{0,1:T(8,128)}) %all-gather.11.cloned.1.call-update) | async-done | bytes 1572880 | tf_op jit(solution)/shard_map/all_gather | solution.py:52
  790.4 3.7 convolution_bitcast_fusion
  794.7 3.7 collective-permute-start.42
  802.8 2.4 collective-permute-start.47
  807.9 3.1 collective-permute-start.46
  811.0 4.3 collective-permute-start.44
  821.3 78.8 %all-reduce = (f32[64]{0:T(128)S(1)}, f32[64]{0:T(128)S(1)}) all-reduce(f32[64]{0:T(128)S(1)} %get-tuple-element.8, f32[64]{0:T(128)S(1)} %fusion.17), channel_id=1, replica_groups=mesh['gx'=4,'gy'=4,'gz'=16] {'gx','gy','gz'}, use_global_device_ids=true, to_apply=%region_7.10 | all-reduce | flops 128 | bytes 1024 | tf_op jit(solution)/shard_map/psum | solution.py:80
  900.8 2.1 multiply_subtract_fusion
  (196 shorter events, 57.3 us)
Async XLA Ops:
  7.2 202.9 %copy-start = (f32[24,6144]{1,0:T(8,128)S(1)}, f32[24,6144]{1,0:T(8,128)}, u32[]{:S(2)}) copy-start(f32[24,6144]{1,0:T(8,128)} %param.18) | copy-start | bytes 1769476
  7.2 202.9 %all-gather.5.cloned.1.call-start = ((), (), s32[]{:S(2)}) async-start(), calls=%async_computation | async-start | bytes 3158016 | tf_op jit(solution)/shard_map/all_gather | solution.py:52
  63.4 5.1 copy-start.2
  66.3 2.2 copy-start.1
  68.4 28.5 %copy-start.3 = (f32[1,1,1,1536,24]{3,4,2,1,0:T(8,128)S(1)}, f32[1,1,1,1536,24]{3,4,2,1,0:T(8,128)}, u32[]{:S(2)}) copy-start(f32[1,1,1,1536,24]{3,4,2,1,0:T(8,128)} %param.17) | copy-start | bytes 442372
  70.4 5.3 collective-permute-start
  75.7 5.3 collective-permute-start.1
  77.1 4.4 collective-permute-start.2
  81.5 7.1 collective-permute-start.3
  82.8 7.1 collective-permute-start.4
  90.0 6.2 collective-permute-start.5
  98.1 294.3 %all-gather.7.cloned.1.call-start = ((), (), s32[]{:S(2)}) async-start(), calls=%async_computation.1 | async-start | bytes 3158016 | tf_op jit(solution)/shard_map/all_gather | solution.py:52
  214.4 31.2 %collective-permute-start.6 = (f32[1,64,256]{2,1,0:T(8,128)S(1)}, f32[1,64,256]{2,1,0:T(8,128)S(1)}, u32[]{:S(2)}, u32[]{:S(2)}) collective-permute-start(f32[1,64,256]{2,1,0:T(8,128)S(1)} %get-tuple-element.61), channel_id=1, source_target_pairs={{0,64},{64,128},{128,192},{1,65},{65,129},{129,193},{2,66},{66,130... | collective-permute-start | bytes 196616 | tf_op jit(solution)/shard_map/ppermute | solution.py:18
  224.0 13.3 %copy-start.11 = (f32[1,1,1,1536]{3,2,1,0:T(1,128)S(1)}, f32[1,1,1,1536]{3,2,1,0:T(1,128)}, u32[]{:S(2)}) copy-start(f32[1,1,1,1536]{3,2,1,0:T(1,128)} %param.15) | copy-start | bytes 18436
  237.4 13.9 %collective-permute-start.11 = (f32[1,64,256]{2,1,0:T(8,128)S(1)}, f32[1,64,256]{2,1,0:T(8,128)S(1)}, u32[]{:S(2)}, u32[]{:S(2)}) collective-permute-start(f32[1,64,256]{2,1,0:T(8,128)S(1)} %get-tuple-element.56), channel_id=1, source_target_pairs={{1,0},{2,1},{3,2},{4,3},{5,4},{6,5},{7,6},{8,7},{9,8},{10,9},{11,1... | collective-permute-start | bytes 196616 | tf_op jit(solution)/shard_map/ppermute | solution.py:20
  239.9 10.0 %collective-permute-start.7 = (f32[1,64,256]{2,1,0:T(8,128)S(1)}, f32[1,64,256]{2,1,0:T(8,128)S(1)}, u32[]{:S(2)}, u32[]{:S(2)}) collective-permute-start(f32[1,64,256]{2,1,0:T(8,128)S(1)} %get-tuple-element.57), channel_id=1, source_target_pairs={{64,0},{128,64},{192,128},{65,1},{129,65},{193,129},{66,2},{130,66... | collective-permute-start | bytes 196616 | tf_op jit(solution)/shard_map/ppermute | solution.py:20
  241.2 10.1 %collective-permute-start.9 = (f32[1,64,256]{2,1,0:T(8,128)S(1)}, f32[1,64,256]{2,1,0:T(8,128)S(1)}, u32[]{:S(2)}, u32[]{:S(2)}) collective-permute-start(f32[1,64,256]{2,1,0:T(8,128)S(1)} %get-tuple-element.58), channel_id=1, source_target_pairs={{16,0},{32,16},{48,32},{17,1},{33,17},{49,33},{18,2},{34,18},{50,3... | collective-permute-start | bytes 196616 | tf_op jit(solution)/shard_map/ppermute | solution.py:20
  242.5 8.8 collective-permute-start.10
  245.6 5.7 collective-permute-start.8
  255.3 144.3 %copy-start.12 = (f32[2]{0:T(128)S(1)}, f32[2]{0:T(128)}, u32[]{:S(2)}) copy-start(f32[2]{0:T(128)} %param.19) | copy-start | bytes 28
  255.6 6.0 collective-permute-start.12
  261.7 6.1 collective-permute-start.13
  263.0 4.8 collective-permute-start.14
  267.8 5.9 collective-permute-start.15
  269.2 5.9 collective-permute-start.16
  275.1 6.2 collective-permute-start.17
  282.4 340.5 %all-gather.9.cloned.1.call-start = ((), (), s32[]{:S(2)}) async-start(), calls=%async_computation.2 | async-start | bytes 3158016 | tf_op jit(solution)/shard_map/all_gather | solution.py:52
  396.6 11.8 %collective-permute-start.18 = (f32[1,64,256]{2,1,0:T(8,128)S(1)}, f32[1,64,256]{2,1,0:T(8,128)S(1)}, u32[]{:S(2)}, u32[]{:S(2)}) collective-permute-start(f32[1,64,256]{2,1,0:T(8,128)S(1)} %get-tuple-element.55), channel_id=1, source_target_pairs={{0,64},{64,128},{128,192},{1,65},{65,129},{129,193},{2,66},{66,130... | collective-permute-start | bytes 196616 | tf_op jit(solution)/shard_map/ppermute | solution.py:18
  400.3 13.9 %collective-permute-start.23 = (f32[1,64,256]{2,1,0:T(8,128)S(1)}, f32[1,64,256]{2,1,0:T(8,128)S(1)}, u32[]{:S(2)}, u32[]{:S(2)}) collective-permute-start(f32[1,64,256]{2,1,0:T(8,128)S(1)} %get-tuple-element.50), channel_id=1, source_target_pairs={{1,0},{2,1},{3,2},{4,3},{5,4},{6,5},{7,6},{8,7},{9,8},{10,9},{11,1... | collective-permute-start | bytes 196616 | tf_op jit(solution)/shard_map/ppermute | solution.py:20
  402.7 10.0 %collective-permute-start.19 = (f32[1,64,256]{2,1,0:T(8,128)S(1)}, f32[1,64,256]{2,1,0:T(8,128)S(1)}, u32[]{:S(2)}, u32[]{:S(2)}) collective-permute-start(f32[1,64,256]{2,1,0:T(8,128)S(1)} %get-tuple-element.51), channel_id=1, source_target_pairs={{64,0},{128,64},{192,128},{65,1},{129,65},{193,129},{66,2},{130,66... | collective-permute-start | bytes 196616 | tf_op jit(solution)/shard_map/ppermute | solution.py:20
  404.0 10.1 %collective-permute-start.21 = (f32[1,64,256]{2,1,0:T(8,128)S(1)}, f32[1,64,256]{2,1,0:T(8,128)S(1)}, u32[]{:S(2)}, u32[]{:S(2)}) collective-permute-start(f32[1,64,256]{2,1,0:T(8,128)S(1)} %get-tuple-element.52), channel_id=1, source_target_pairs={{16,0},{32,16},{48,32},{17,1},{33,17},{49,33},{18,2},{34,18},{50,3... | collective-permute-start | bytes 196616 | tf_op jit(solution)/shard_map/ppermute | solution.py:20
  405.3 8.8 collective-permute-start.22
  408.4 5.7 collective-permute-start.20
  496.0 13.4 %copy-start.9 = (f32[64]{0:T(128)}, f32[64]{0:T(128)S(1)}, u32[]{:S(2)}) copy-start(f32[64]{0:T(128)S(1)} %add_divide_fusion.1) | copy-start | bytes 772
  499.9 9.5 %collective-permute-start.24 = (f32[1,64,256]{2,1,0:T(8,128)S(1)}, f32[1,64,256]{2,1,0:T(8,128)S(1)}, u32[]{:S(2)}, u32[]{:S(2)}) collective-permute-start(f32[1,64,256]{2,1,0:T(8,128)S(1)} %get-tuple-element.49), channel_id=1, source_target_pairs={{0,64},{64,128},{128,192},{1,65},{65,129},{129,193},{2,66},{66,130... | collective-permute-start | bytes 196616 | tf_op jit(solution)/shard_map/ppermute | solution.py:18
  501.2 14.4 %collective-permute-start.29 = (f32[1,64,256]{2,1,0:T(8,128)S(1)}, f32[1,64,256]{2,1,0:T(8,128)S(1)}, u32[]{:S(2)}, u32[]{:S(2)}) collective-permute-start(f32[1,64,256]{2,1,0:T(8,128)S(1)} %get-tuple-element.44), channel_id=1, source_target_pairs={{1,0},{2,1},{3,2},{4,3},{5,4},{6,5},{7,6},{8,7},{9,8},{10,9},{11,1... | collective-permute-start | bytes 196616 | tf_op jit(solution)/shard_map/ppermute | solution.py:20
  504.1 9.6 %collective-permute-start.25 = (f32[1,64,256]{2,1,0:T(8,128)S(1)}, f32[1,64,256]{2,1,0:T(8,128)S(1)}, u32[]{:S(2)}, u32[]{:S(2)}) collective-permute-start(f32[1,64,256]{2,1,0:T(8,128)S(1)} %get-tuple-element.45), channel_id=1, source_target_pairs={{64,0},{128,64},{192,128},{65,1},{129,65},{193,129},{66,2},{130,66... | collective-permute-start | bytes 196616 | tf_op jit(solution)/shard_map/ppermute | solution.py:20
  505.4 10.2 %collective-permute-start.27 = (f32[1,64,256]{2,1,0:T(8,128)S(1)}, f32[1,64,256]{2,1,0:T(8,128)S(1)}, u32[]{:S(2)}, u32[]{:S(2)}) collective-permute-start(f32[1,64,256]{2,1,0:T(8,128)S(1)} %get-tuple-element.46), channel_id=1, source_target_pairs={{16,0},{32,16},{48,32},{17,1},{33,17},{49,33},{18,2},{34,18},{50,3... | collective-permute-start | bytes 196616 | tf_op jit(solution)/shard_map/ppermute | solution.py:20
  506.7 8.9 collective-permute-start.28
  509.4 6.2 collective-permute-start.26
  516.8 273.6 %all-gather.11.cloned.1.call-start = ((), (), s32[]{:S(2)}) async-start(), calls=%async_computation.3 | async-start | bytes 3158016 | tf_op jit(solution)/shard_map/all_gather | solution.py:52
  627.1 11.2 %collective-permute-start.30 = (f32[1,64,256]{2,1,0:T(8,128)S(1)}, f32[1,64,256]{2,1,0:T(8,128)S(1)}, u32[]{:S(2)}, u32[]{:S(2)}) collective-permute-start(f32[1,64,256]{2,1,0:T(8,128)S(1)} %get-tuple-element.43), channel_id=1, source_target_pairs={{0,64},{64,128},{128,192},{1,65},{65,129},{129,193},{2,66},{66,130... | collective-permute-start | bytes 196616 | tf_op jit(solution)/shard_map/ppermute | solution.py:18
  630.2 13.9 %collective-permute-start.35 = (f32[1,64,256]{2,1,0:T(8,128)S(1)}, f32[1,64,256]{2,1,0:T(8,128)S(1)}, u32[]{:S(2)}, u32[]{:S(2)}) collective-permute-start(f32[1,64,256]{2,1,0:T(8,128)S(1)} %get-tuple-element.38), channel_id=1, source_target_pairs={{1,0},{2,1},{3,2},{4,3},{5,4},{6,5},{7,6},{8,7},{9,8},{10,9},{11,1... | collective-permute-start | bytes 196616 | tf_op jit(solution)/shard_map/ppermute | solution.py:20
  632.6 10.0 %collective-permute-start.31 = (f32[1,64,256]{2,1,0:T(8,128)S(1)}, f32[1,64,256]{2,1,0:T(8,128)S(1)}, u32[]{:S(2)}, u32[]{:S(2)}) collective-permute-start(f32[1,64,256]{2,1,0:T(8,128)S(1)} %get-tuple-element.39), channel_id=1, source_target_pairs={{64,0},{128,64},{192,128},{65,1},{129,65},{193,129},{66,2},{130,66... | collective-permute-start | bytes 196616 | tf_op jit(solution)/shard_map/ppermute | solution.py:20
  633.9 10.1 %collective-permute-start.33 = (f32[1,64,256]{2,1,0:T(8,128)S(1)}, f32[1,64,256]{2,1,0:T(8,128)S(1)}, u32[]{:S(2)}, u32[]{:S(2)}) collective-permute-start(f32[1,64,256]{2,1,0:T(8,128)S(1)} %get-tuple-element.40), channel_id=1, source_target_pairs={{16,0},{32,16},{48,32},{17,1},{33,17},{49,33},{18,2},{34,18},{50,3... | collective-permute-start | bytes 196616 | tf_op jit(solution)/shard_map/ppermute | solution.py:20
  635.2 8.8 collective-permute-start.34
  638.4 5.7 collective-permute-start.32
  644.1 6.8 copy-start.4
  653.7 6.0 collective-permute-start.36
  659.8 6.1 collective-permute-start.37
  661.1 4.8 collective-permute-start.38
  666.0 5.9 collective-permute-start.39
  667.3 5.9 collective-permute-start.40
  673.2 6.2 collective-permute-start.41
  679.4 111.1 %copy-start.6 = (f32[64,6,256]{2,0,1:T(8,128)}, f32[64,6,256]{2,0,1:T(8,128)S(1)}, u32[]{:S(2)}) copy-start(f32[64,6,256]{2,0,1:T(8,128)S(1)} %constant_dynamic-update-slice_fusion.36) | copy-start | bytes 1179652
  794.7 16.2 %collective-permute-start.42 = (f32[1,64,256]{2,1,0:T(8,128)S(1)}, f32[1,64,256]{2,1,0:T(8,128)}, u32[]{:S(2)}, u32[]{:S(2)}) collective-permute-start(f32[1,64,256]{2,1,0:T(8,128)S(1)} %get-tuple-element.37), channel_id=1, source_target_pairs={{0,64},{64,128},{128,192},{1,65},{65,129},{129,193},{2,66},{66,130... | collective-permute-start | bytes 196616 | tf_op jit(solution)/shard_map/ppermute | solution.py:18
  799.5 20.5 %copy-start.10 = (f32[64]{0:T(128)S(1)}, f32[64]{0:T(128)}, u32[]{:S(2)}) copy-start(f32[64]{0:T(128)} %copy-done.9) | copy-start | bytes 772
  801.7 99.1 %copy-start.7 = (f32[1,1,1,64,1536]{4,3,2,1,0:T(8,128)S(1)}, f32[1,1,1,64,1536]{4,3,2,1,0:T(8,128)}, u32[]{:S(2)}) copy-start(f32[1,1,1,64,1536]{4,3,2,1,0:T(8,128)} %sub.78) | copy-start | bytes 1179652
  802.8 13.9 %collective-permute-start.47 = (f32[1,64,256]{2,1,0:T(8,128)S(1)}, f32[1,64,256]{2,1,0:T(8,128)S(1)}, u32[]{:S(2)}, u32[]{:S(2)}) collective-permute-start(f32[1,64,256]{2,1,0:T(8,128)S(1)} %get-tuple-element.32), channel_id=1, source_target_pairs={{1,0},{2,1},{3,2},{4,3},{5,4},{6,5},{7,6},{8,7},{9,8},{10,9},{11,1... | collective-permute-start | bytes 196616 | tf_op jit(solution)/shard_map/ppermute | solution.py:20
  805.3 10.9 %collective-permute-start.43 = (f32[1,64,256]{2,1,0:T(8,128)S(1)}, f32[1,64,256]{2,1,0:T(8,128)S(1)}, u32[]{:S(2)}, u32[]{:S(2)}) collective-permute-start(f32[1,64,256]{2,1,0:T(8,128)S(1)} %get-tuple-element.33), channel_id=1, source_target_pairs={{64,0},{128,64},{192,128},{65,1},{129,65},{193,129},{66,2},{130,66... | collective-permute-start | bytes 196616 | tf_op jit(solution)/shard_map/ppermute | solution.py:20
  806.6 10.1 %collective-permute-start.45 = (f32[1,64,256]{2,1,0:T(8,128)S(1)}, f32[1,64,256]{2,1,0:T(8,128)S(1)}, u32[]{:S(2)}, u32[]{:S(2)}) collective-permute-start(f32[1,64,256]{2,1,0:T(8,128)S(1)} %get-tuple-element.34), channel_id=1, source_target_pairs={{16,0},{32,16},{48,32},{17,1},{33,17},{49,33},{18,2},{34,18},{50,3... | collective-permute-start | bytes 196616 | tf_op jit(solution)/shard_map/ppermute | solution.py:20
  807.9 8.8 collective-permute-start.46
  811.0 5.7 collective-permute-start.44
  816.7 84.0 %copy-start.8 = (f32[1,1,1,64,1536]{4,3,2,1,0:T(8,128)S(1)}, f32[1,1,1,64,1536]{4,3,2,1,0:T(8,128)}, u32[]{:S(2)}) copy-start(f32[1,1,1,64,1536]{4,3,2,1,0:T(8,128)} %sub.86) | copy-start | bytes 1179652
  (1 other events, 0.8 us)
Sparse Core Ops, SparseCore 0:
  98.2 111.8 all-gather.4
  282.5 109.7 all-gather.6
  516.9 105.8 all-gather.8
  680.6 109.7 all-gather.10
where the time goes:
time: 912 us; the launch traced here: 909 us
  waiting for transfers between devices  468 us (51%)
  blocking collectives  159 us (17%)
  starting transfers between devices  129 us (14%)
  local copies, waits for them, and re-layouts  80.7 us (9%)
  matrix products  35.1 us (4%)
  other arithmetic  22.8 us (2%)
  between operations  15.2 us (2%)
    all_gather x4, waiting for transfers between devices, project(): lax.all_gather(weights, ('gx', 'gy', 'gz'), axis=1, tiled=True)  438 us
    psum x2, blocking collectives, shards(): lax.psum((jnp.sum(residual * image, axis=1), jnp.sum(image * image, axis=...  159 us
    ppermute x24, starting transfers between devices, extended(): lax.ppermute(tail, axis, [(i, (i + 1) % count) for i in range(ends)])  87.9 us
    ppermute x24, starting transfers between devices, extended(): lax.ppermute(head, axis, [((i + 1) % count, i) for i in range(ends)])  41.2 us
    gather x2, local copies, waits for them, and re-layouts, reorder(): return jnp.take(rows, order, axis=1)  26.7 us
    gather x2, local copies, waits for them, and re-layouts, reorder(): rows = jnp.take(matrix, order, axis=0)  26.7 us
  transfers between devices with their start and end apart: 52, of which 22 were waited for; matrix products, arithmetic and copies ran while one was open for 3% of the time, Pallas kernels for 0%

commit v1 on v0

--- a/solution.py
+++ b/solution.py
@@ -49,7 +49,12 @@
 def project(field, basis, coarse_rows):
     weights = jnp.dot(field, basis, precision=HIGH)
     share = jnp.dot(
-        lax.all_gather(weights, ("gx", "gy", "gz"), axis=1, tiled=True),
+        jnp.concatenate(
+            lax.all_to_all(
+                jnp.stack([weights] * lax.axis_size(("gx", "gy", "gz"))), ("gx", "gy", "gz"), 0, 0
+            ),
+            axis=1,
+        ),
         coarse_rows.T,
         precision=HIGH,
     )

time: 912 us -> 738 us (0.81)
  waiting for transfers between devices: 468 us -> 73.1 us
  blocking collectives: 159 us -> 319 us
  local copies, waits for them, and re-layouts: 80.7 us -> 110 us
  other arithmetic: 22.8 us -> 44 us
  starting transfers between devices: 129 us -> 146 us
  between operations: 15.2 us -> 2.56 us
    all_gather x4 -> x0, waiting for transfers between devices: 438 us -> none  [project(): lax.all_gather(weights, ('gx', 'gy', 'gz'), axis=1, tiled=True)]
    all_to_all x0 -> x3, blocking collectives: none -> 168 us  [project(): lax.all_to_all(jnp.stack([weights] * lax.axis_size(('gx', 'gy', 'gz'))),...]
    all_to_all x0 -> x1, waiting for transfers between devices: none -> 43.6 us  [project(): lax.all_to_all(jnp.stack([weights] * lax.axis_size(('gx', 'gy', 'gz'))),...]
    unnamed x35 -> x71, local copies, waits for them, and re-layouts: 3.03 us -> 37.4 us
    all_to_all x0 -> x4, other arithmetic: none -> 23.3 us  [project(): lax.all_to_all(jnp.stack([weights] * lax.axis_size(('gx', 'gy', 'gz'))),...]
    all_to_all x0 -> x1, starting transfers between devices: none -> 18.1 us  [project(): lax.all_to_all(jnp.stack([weights] * lax.axis_size(('gx', 'gy', 'gz'))),...]
  transfers between devices with their start and end apart: 52 -> 49, of which waited for: 22 -> 21; matrix products, arithmetic and copies ran while one was open for 3% -> 3% of each run, Pallas kernels for 0% -> 0%
where the time goes in v1:
time: 738 us; the launch traced here: 727 us
  blocking collectives  319 us (43%)
  starting transfers between devices  146 us (20%)
  local copies, waits for them, and re-layouts  110 us (15%)
  waiting for transfers between devices  73.1 us (10%)
  other arithmetic  44 us (6%)
  matrix products  32 us (4%)
    all_to_all x3, blocking collectives, project(): lax.all_to_all(jnp.stack([weights] * lax.axis_size(('gx', 'gy', 'gz'))),...  168 us
    psum x2, blocking collectives, shards(): lax.psum((jnp.sum(residual * image, axis=1), jnp.sum(image * image, axis=...  151 us
    ppermute x24, starting transfers between devices, extended(): lax.ppermute(tail, axis, [(i, (i + 1) % count) for i in range(ends)])  90.2 us
    all_to_all x1, waiting for transfers between devices, project(): lax.all_to_all(jnp.stack([weights] * lax.axis_size(('gx', 'gy', 'gz'))),...  43.6 us
    ppermute x24, starting transfers between devices, extended(): lax.ppermute(head, axis, [((i + 1) % count, i) for i in range(ends)])  37.5 us
    unnamed x71, local copies, waits for them, and re-layouts  37.4 us
    gather x2, local copies, waits for them, and re-layouts, reorder(): return jnp.take(rows, order, axis=1)  26.7 us
    gather x2, local copies, waits for them, and re-layouts, reorder(): rows = jnp.take(matrix, order, axis=0)  26.7 us
  transfers between devices with their start and end apart: 49, of which 21 were waited for; matrix products, arithmetic and copies ran while one was open for 3% of the time, Pallas kernels for 0%

profile of v1, /device:TPU:1, one launch (start us, length us, event | category | flops | bytes accessed | tf_op | source)
XLA Modules:
  0.0 727.0 jit_solution(18042276230818023962)
XLA Ops:
  1.5 13.4 %gather_fusion.2 = bf16[1536,1536]{1,0:T(8,128)(2,1)} fusion(bf16[1536,1536]{1,0:T(8,128)(2,1)} %bitcast.423, s32[2048]{0:T(1024)S(1)} %pad_clamp_fusion), kind=kCustom, calls=%fused_computation.2.clone | custom fusion | bytes 9443328 | tf_op jit(solution)/shard_map/jit(_take)/gather | solution.py:28
  14.8 13.3 %gather_fusion = bf16[1536,1536]{1,0:T(8,128)(2,1)} fusion(bf16[1536,1536]{1,0:T(8,128)(2,1)} %bitcast.424, s32[2048]{0:T(1024)S(1)} %pad_clamp_fusion), kind=kCustom, calls=%fused_computation.clone | custom fusion | bytes 9443328 | tf_op jit(solution)/shard_map/jit(_take)/gather | solution.py:28
  28.1 8.7 %broadcast_select_fusion = (bf16[1536,1536]{1,0:T(8,128)(2,1)}, bf16[1536,1536]{1,0:T(8,128)(2,1)}) fusion(bf16[1536,1536]{1,0:T(8,128)(2,1)} %gather_fusion.2, pred[1536]{0:T(1024)(128)(4,1)S(1)} %compare_and_fusion, bf16[1536,1536]{1,0:T(8,128)(2,1)} %gather_fusion), kind=kLoop, calls=%fused_computation.10 | loop fusion | flops 4718592 | bytes 18875904 | tf_op jit(solution)/shard_map/jit(_take)/select_n | solution.py:28
  36.8 6.6 copy.40
  43.5 13.4 %gather_fusion.1 = bf16[1536,1536]{1,0:T(8,128)(2,1)} fusion(bf16[1536,1536]{0,1:T(8,128)(2,1)} %copy.40, s32[2048]{0:T(1024)S(1)} %pad_clamp_fusion), kind=kCustom, calls=%fused_computation.1.clone | custom fusion | bytes 9443328 | tf_op jit(solution)/shard_map/jit(_take)/gather | solution.py:29
  56.8 2.9 broadcast_select_fusion.3
  59.7 2.2 copy-done.1
  63.9 4.0 collective-permute-start
  70.5 3.1 collective-permute-start.2
  76.3 5.8 collective-permute-start.4
  83.4 2.4 collective-permute-start.5
  85.8 3.8 collective-permute-done.5
  92.1 4.4 reshape.374
  96.6 18.1 %all-to-all-start = ((f32[256,1,1536]{2,1,0:T(1,128)}), f32[256,1,1536]{2,1,0:T(1,128)S(1)}, u32[]{:S(2)}, u32[]{:S(2)}) async-start(f32[256,1,1536]{2,1,0:T(1,128)} %reshape.374), calls=%async_computation | async-start | bytes 3145728 | tf_op jit(solution)/shard_map/all_to_all | solution.py:53
  114.8 43.6 %all-to-all-done = f32[256,1,1536]{2,1,0:T(1,128)S(1)} async-done(((f32[256,1,1536]{2,1,0:T(1,128)}), f32[256,1,1536]{2,1,0:T(1,128)S(1)}, u32[]{:S(2)}, u32[]{:S(2)}) %all-to-all-start) | async-done | bytes 1572896 | tf_op jit(solution)/shard_map/all_to_all | solution.py:53
  159.0 5.9 reduce.4
  164.8 3.4 reshape.375
  168.2 3.7 convolution_bitcast_fusion.3
  172.5 2.3 collective-permute-start.6
  174.8 6.7 copy.50
  181.5 13.4 %gather_fusion.3 = bf16[1536,1536]{1,0:T(8,128)(2,1)} fusion(bf16[1536,1536]{0,1:T(8,128)(2,1)} %copy.50, s32[2048]{0:T(1024)S(1)} %pad_clamp_fusion), kind=kCustom, calls=%fused_computation.3.clone | custom fusion | bytes 9443328 | tf_op jit(solution)/shard_map/jit(_take)/gather | solution.py:29
  199.4 3.6 collective-permute-start.10
  203.0 4.7 collective-permute-start.8
  208.8 3.9 fusion.6
  213.1 4.3 collective-permute-start.12
  220.1 4.0 collective-permute-start.14
  226.8 5.0 collective-permute-start.16
  235.0 4.3 collective-permute-done.17
  242.0 3.5 reshape.376
  245.5 56.5 %all_to_all.20 = f32[256,1,1536]{2,1,0:T(1,128)} all-to-all(f32[256,1,1536]{2,1,0:T(1,128)S(1)} %reshape.376), channel_id=1, replica_groups=mesh['gx'=4,'gy'=4,'gz'=16] {'gx','gy','gz'}, dimensions={0} | all-to-all | bytes 3145728 | tf_op jit(solution)/shard_map/all_to_all | solution.py:53
  302.0 5.8 reduce.5
  307.8 2.1 reshape.377
  309.9 3.8 convolution_bitcast_fusion.2
  314.3 2.3 collective-permute-start.18
  321.6 3.6 collective-permute-start.22
  325.3 4.4 collective-permute-start.20
  332.4 75.9 %all-reduce.1 = (f32[64]{0:T(128)S(1)}, f32[64]{0:T(128)S(1)}) all-reduce(f32[64]{0:T(128)S(1)} %get-tuple-element.12, f32[64]{0:T(128)S(1)} %get-tuple-element.10), channel_id=1, replica_groups=mesh['gx'=4,'gy'=4,'gz'=16] {'gx','gy','gz'}, use_global_device_ids=true, to_apply=%region_3.6 | all-reduce | flops 128 | bytes 1024 | tf_op jit(solution)/shard_map/psum | solution.py:85
  409.0 3.9 fusion.18
  414.2 2.9 collective-permute-start.29
  419.7 3.2 collective-permute-start.28
  422.9 4.3 collective-permute-start.26
  431.3 3.5 reshape.378
  434.8 54.8 %all_to_all.21 = f32[256,1,1536]{2,1,0:T(1,128)} all-to-all(f32[256,1,1536]{2,1,0:T(1,128)S(1)} %reshape.378), channel_id=1, replica_groups=mesh['gx'=4,'gy'=4,'gz'=16] {'gx','gy','gz'}, dimensions={0} | all-to-all | bytes 3145728 | tf_op jit(solution)/shard_map/all_to_all | solution.py:53
  489.6 5.8 reduce.6
  495.4 2.0 reshape.379
  497.4 3.8 convolution_bitcast_fusion.1
  501.7 2.3 collective-permute-start.30
  508.5 3.6 collective-permute-start.34
  512.2 4.3 collective-permute-start.32
  517.9 3.9 fusion.9
  522.3 4.3 collective-permute-start.36
  529.3 4.0 collective-permute-start.38
  536.0 4.9 collective-permute-start.40
  542.2 2.0 collective-permute-start.41
  544.2 4.2 collective-permute-done.41
  550.8 4.4 reshape.380
  555.2 56.8 %all_to_all.22 = f32[256,1,1536]{2,1,0:T(1,128)S(1)} all-to-all(f32[256,1,1536]{2,1,0:T(1,128)} %reshape.380), channel_id=1, replica_groups=mesh['gx'=4,'gy'=4,'gz'=16] {'gx','gy','gz'}, dimensions={0} | all-to-all | bytes 3145728 | tf_op jit(solution)/shard_map/all_to_all | solution.py:53
  612.0 5.9 reduce.7
  617.9 3.4 reshape.381
  621.3 3.8 convolution_bitcast_fusion
  626.4 2.9 collective-permute-start.42
  636.5 3.6 collective-permute-start.46
  640.1 4.3 collective-permute-start.44
  649.8 75.1 %all-reduce = (f32[64]{0:T(128)S(1)}, f32[64]{0:T(128)S(1)}) all-reduce(f32[64]{0:T(128)S(1)} %get-tuple-element.8, f32[64]{0:T(128)S(1)} %fusion.17), channel_id=1, replica_groups=mesh['gx'=4,'gy'=4,'gz'=16] {'gx','gy','gz'}, use_global_device_ids=true, to_apply=%region_7.10 | all-reduce | flops 128 | bytes 1024 | tf_op jit(solution)/shard_map/psum | solution.py:85
  (230 shorter events, 77.9 us)
Async XLA Ops:
  0.6 167.6 %copy-start = (f32[24,6144]{1,0:T(8,128)S(1)}, f32[24,6144]{1,0:T(8,128)}, u32[]{:S(2)}) copy-start(f32[24,6144]{1,0:T(8,128)} %param.18) | copy-start | bytes 1769476
  61.9 27.8 %copy-start.3 = (f32[1,1,1,1536,24]{3,4,2,1,0:T(8,128)S(1)}, f32[1,1,1,1536,24]{3,4,2,1,0:T(8,128)}, u32[]{:S(2)}) copy-start(f32[1,1,1,1536,24]{3,4,2,1,0:T(8,128)} %param.17) | copy-start | bytes 442372
  63.9 5.3 collective-permute-start
  69.2 5.3 collective-permute-start.1
  70.5 4.4 collective-permute-start.2
  75.0 7.1 collective-permute-start.3
  76.3 7.1 collective-permute-start.4
  83.4 6.2 collective-permute-start.5
  96.6 61.8 %all-to-all-start = ((f32[256,1,1536]{2,1,0:T(1,128)}), f32[256,1,1536]{2,1,0:T(1,128)S(1)}, u32[]{:S(2)}, u32[]{:S(2)}) async-start(f32[256,1,1536]{2,1,0:T(1,128)} %reshape.374), calls=%async_computation | async-start | bytes 3145728 | tf_op jit(solution)/shard_map/all_to_all | solution.py:53
  114.7 386.4 %copy-start.4 = (f32[6,256,24]{1,0,2:T(8,128)}, f32[6,256,24]{1,0,2:T(8,128)S(1)}, u32[]{:S(2)}) copy-start(f32[6,256,24]{1,0,2:T(8,128)S(1)} %dot_general.60) | copy-start | bytes 442372
  164.8 9.9 %copy-start.23 = (f32[1,1,1,1536]{3,2,1,0:T(1,128)S(1)}, f32[1,1,1,1536]{3,2,1,0:T(1,128)}, u32[]{:S(2)}) copy-start(f32[1,1,1,1536]{3,2,1,0:T(1,128)} %param.15) | copy-start | bytes 18436
  172.5 30.5 %collective-permute-start.6 = (f32[1,64,256]{2,1,0:T(8,128)S(1)}, f32[1,64,256]{2,1,0:T(8,128)S(1)}, u32[]{:S(2)}, u32[]{:S(2)}) collective-permute-start(f32[1,64,256]{2,1,0:T(8,128)S(1)} %get-tuple-element.61), channel_id=1, source_target_pairs={{0,64},{64,128},{128,192},{1,65},{65,129},{129,193},{2,66},{66,130... | collective-permute-start | bytes 196616 | tf_op jit(solution)/shard_map/ppermute | solution.py:18
  181.5 27.3 %copy-start.18 = (f32[6,8,8,256]{3,2,0,1:T(8,128)S(1)}, f32[6,8,8,256]{3,2,0,1:T(8,128)}, u32[]{:S(2)}) copy-start(f32[6,8,8,256]{3,2,0,1:T(8,128)} %copy-done.17) | copy-start | bytes 1179652
  194.8 13.8 %collective-permute-start.11 = (f32[1,64,256]{2,1,0:T(8,128)S(1)}, f32[1,64,256]{2,1,0:T(8,128)S(1)}, u32[]{:S(2)}, u32[]{:S(2)}) collective-permute-start(f32[1,64,256]{2,1,0:T(8,128)S(1)} %get-tuple-element.56), channel_id=1, source_target_pairs={{1,0},{2,1},{3,2},{4,3},{5,4},{6,5},{7,6},{8,7},{9,8},{10,9},{11,1... | collective-permute-start | bytes 196616 | tf_op jit(solution)/shard_map/ppermute | solution.py:20
  196.8 11.0 %collective-permute-start.7 = (f32[1,64,256]{2,1,0:T(8,128)S(1)}, f32[1,64,256]{2,1,0:T(8,128)S(1)}, u32[]{:S(2)}, u32[]{:S(2)}) collective-permute-start(f32[1,64,256]{2,1,0:T(8,128)S(1)} %get-tuple-element.57), channel_id=1, source_target_pairs={{64,0},{128,64},{192,128},{65,1},{129,65},{193,129},{66,2},{130,66... | collective-permute-start | bytes 196616 | tf_op jit(solution)/shard_map/ppermute | solution.py:20
  198.1 10.6 %collective-permute-start.9 = (f32[1,64,256]{2,1,0:T(8,128)S(1)}, f32[1,64,256]{2,1,0:T(8,128)S(1)}, u32[]{:S(2)}, u32[]{:S(2)}) collective-permute-start(f32[1,64,256]{2,1,0:T(8,128)S(1)} %get-tuple-element.58), channel_id=1, source_target_pairs={{16,0},{32,16},{48,32},{17,1},{33,17},{49,33},{18,2},{34,18},{50,3... | collective-permute-start | bytes 196616 | tf_op jit(solution)/shard_map/ppermute | solution.py:20
  199.4 9.3 %collective-permute-start.10 = (f32[1,64,256]{2,1,0:T(8,128)S(1)}, f32[1,64,256]{2,1,0:T(8,128)S(1)}, u32[]{:S(2)}, u32[]{:S(2)}) collective-permute-start(f32[1,64,256]{2,1,0:T(8,128)S(1)} %get-tuple-element.59), channel_id=1, source_target_pairs={{0,1},{1,2},{2,3},{3,4},{4,5},{5,6},{6,7},{7,8},{8,9},{9,10},{10,1... | collective-permute-start | bytes 196616 | tf_op jit(solution)/shard_map/ppermute | solution.py:18
  203.0 5.6 collective-permute-start.8
  213.1 5.7 collective-permute-start.12
  218.8 6.1 collective-permute-start.13
  220.1 5.3 collective-permute-start.14
  225.4 6.3 collective-permute-start.15
  226.8 6.3 collective-permute-start.16
  233.1 6.2 collective-permute-start.17
  307.8 8.7 %copy-start.24 = (f32[2]{0:T(128)S(1)}, f32[2]{0:T(128)}, u32[]{:S(2)}) copy-start(f32[2]{0:T(128)} %param.19) | copy-start | bytes 28
  309.9 21.0 %copy-start.14 = (f32[64,6,256]{2,0,1:T(8,128)S(1)}, f32[64,6,256]{2,0,1:T(8,128)}, u32[]{:S(2)}) copy-start(f32[64,6,256]{2,0,1:T(8,128)} %copy-done.13) | copy-start | bytes 1179652
  314.3 11.0 %collective-permute-start.18 = (f32[1,64,256]{2,1,0:T(8,128)S(1)}, f32[1,64,256]{2,1,0:T(8,128)S(1)}, u32[]{:S(2)}, u32[]{:S(2)}) collective-permute-start(f32[1,64,256]{2,1,0:T(8,128)S(1)} %get-tuple-element.55), channel_id=1, source_target_pairs={{0,64},{64,128},{128,192},{1,65},{65,129},{129,193},{2,66},{66,130... | collective-permute-start | bytes 196616 | tf_op jit(solution)/shard_map/ppermute | solution.py:18
  317.1 13.8 %collective-permute-start.23 = (f32[1,64,256]{2,1,0:T(8,128)S(1)}, f32[1,64,256]{2,1,0:T(8,128)S(1)}, u32[]{:S(2)}, u32[]{:S(2)}) collective-permute-start(f32[1,64,256]{2,1,0:T(8,128)S(1)} %get-tuple-element.50), channel_id=1, source_target_pairs={{1,0},{2,1},{3,2},{4,3},{5,4},{6,5},{7,6},{8,7},{9,8},{10,9},{11,1... | collective-permute-start | bytes 196616 | tf_op jit(solution)/shard_map/ppermute | solution.py:20
  319.0 10.7 %collective-permute-start.19 = (f32[1,64,256]{2,1,0:T(8,128)S(1)}, f32[1,64,256]{2,1,0:T(8,128)S(1)}, u32[]{:S(2)}, u32[]{:S(2)}) collective-permute-start(f32[1,64,256]{2,1,0:T(8,128)S(1)} %get-tuple-element.51), channel_id=1, source_target_pairs={{64,0},{128,64},{192,128},{65,1},{129,65},{193,129},{66,2},{130,66... | collective-permute-start | bytes 196616 | tf_op jit(solution)/shard_map/ppermute | solution.py:20
  320.3 10.6 %collective-permute-start.21 = (f32[1,64,256]{2,1,0:T(8,128)S(1)}, f32[1,64,256]{2,1,0:T(8,128)S(1)}, u32[]{:S(2)}, u32[]{:S(2)}) collective-permute-start(f32[1,64,256]{2,1,0:T(8,128)S(1)} %get-tuple-element.52), channel_id=1, source_target_pairs={{16,0},{32,16},{48,32},{17,1},{33,17},{49,33},{18,2},{34,18},{50,3... | collective-permute-start | bytes 196616 | tf_op jit(solution)/shard_map/ppermute | solution.py:20
  321.6 9.3 %collective-permute-start.22 = (f32[1,64,256]{2,1,0:T(8,128)S(1)}, f32[1,64,256]{2,1,0:T(8,128)S(1)}, u32[]{:S(2)}, u32[]{:S(2)}) collective-permute-start(f32[1,64,256]{2,1,0:T(8,128)S(1)} %get-tuple-element.53), channel_id=1, source_target_pairs={{0,1},{1,2},{2,3},{3,4},{4,5},{5,6},{6,7},{7,8},{8,9},{9,10},{10,1... | collective-permute-start | bytes 196616 | tf_op jit(solution)/shard_map/ppermute | solution.py:18
  325.3 5.6 collective-permute-start.20
  409.0 14.0 %copy-start.21 = (f32[64]{0:T(128)}, f32[64]{0:T(128)S(1)}, u32[]{:S(2)}) copy-start(f32[64]{0:T(128)S(1)} %add_divide_fusion.1) | copy-start | bytes 772
  412.9 10.0 %collective-permute-start.24 = (f32[1,64,256]{2,1,0:T(8,128)S(1)}, f32[1,64,256]{2,1,0:T(8,128)S(1)}, u32[]{:S(2)}, u32[]{:S(2)}) collective-permute-start(f32[1,64,256]{2,1,0:T(8,128)S(1)} %get-tuple-element.49), channel_id=1, source_target_pairs={{0,64},{64,128},{128,192},{1,65},{65,129},{129,193},{2,66},{66,130... | collective-permute-start | bytes 196616 | tf_op jit(solution)/shard_map/ppermute | solution.py:18
  414.2 14.4 %collective-permute-start.29 = (f32[1,64,256]{2,1,0:T(8,128)S(1)}, f32[1,64,256]{2,1,0:T(8,128)S(1)}, u32[]{:S(2)}, u32[]{:S(2)}) collective-permute-start(f32[1,64,256]{2,1,0:T(8,128)S(1)} %get-tuple-element.44), channel_id=1, source_target_pairs={{1,0},{2,1},{3,2},{4,3},{5,4},{6,5},{7,6},{8,7},{9,8},{10,9},{11,1... | collective-permute-start | bytes 196616 | tf_op jit(solution)/shard_map/ppermute | solution.py:20
  417.1 10.1 %collective-permute-start.25 = (f32[1,64,256]{2,1,0:T(8,128)S(1)}, f32[1,64,256]{2,1,0:T(8,128)S(1)}, u32[]{:S(2)}, u32[]{:S(2)}) collective-permute-start(f32[1,64,256]{2,1,0:T(8,128)S(1)} %get-tuple-element.45), channel_id=1, source_target_pairs={{64,0},{128,64},{192,128},{65,1},{129,65},{193,129},{66,2},{130,66... | collective-permute-start | bytes 196616 | tf_op jit(solution)/shard_map/ppermute | solution.py:20
  418.4 10.2 %collective-permute-start.27 = (f32[1,64,256]{2,1,0:T(8,128)S(1)}, f32[1,64,256]{2,1,0:T(8,128)S(1)}, u32[]{:S(2)}, u32[]{:S(2)}) collective-permute-start(f32[1,64,256]{2,1,0:T(8,128)S(1)} %get-tuple-element.46), channel_id=1, source_target_pairs={{16,0},{32,16},{48,32},{17,1},{33,17},{49,33},{18,2},{34,18},{50,3... | collective-permute-start | bytes 196616 | tf_op jit(solution)/shard_map/ppermute | solution.py:20
  419.7 8.9 %collective-permute-start.28 = (f32[1,64,256]{2,1,0:T(8,128)S(1)}, f32[1,64,256]{2,1,0:T(8,128)S(1)}, u32[]{:S(2)}, u32[]{:S(2)}) collective-permute-start(f32[1,64,256]{2,1,0:T(8,128)S(1)} %get-tuple-element.47), channel_id=1, source_target_pairs={{0,1},{1,2},{2,3},{3,4},{4,5},{5,6},{6,7},{7,8},{8,9},{9,10},{10,1... | collective-permute-start | bytes 196616 | tf_op jit(solution)/shard_map/ppermute | solution.py:18
  422.9 5.6 collective-permute-start.26
  497.4 20.5 %copy-start.20 = (f32[6,8,8,256]{3,2,0,1:T(8,128)S(1)}, f32[6,8,8,256]{3,2,0,1:T(8,128)}, u32[]{:S(2)}) copy-start(f32[6,8,8,256]{3,2,0,1:T(8,128)} %copy-done.19) | copy-start | bytes 1179652
  501.7 10.4 %collective-permute-start.30 = (f32[1,64,256]{2,1,0:T(8,128)S(1)}, f32[1,64,256]{2,1,0:T(8,128)S(1)}, u32[]{:S(2)}, u32[]{:S(2)}) collective-permute-start(f32[1,64,256]{2,1,0:T(8,128)S(1)} %get-tuple-element.43), channel_id=1, source_target_pairs={{0,64},{64,128},{128,192},{1,65},{65,129},{129,193},{2,66},{66,130... | collective-permute-start | bytes 196616 | tf_op jit(solution)/shard_map/ppermute | solution.py:18
  504.0 13.9 %collective-permute-start.35 = (f32[1,64,256]{2,1,0:T(8,128)S(1)}, f32[1,64,256]{2,1,0:T(8,128)S(1)}, u32[]{:S(2)}, u32[]{:S(2)}) collective-permute-start(f32[1,64,256]{2,1,0:T(8,128)S(1)} %get-tuple-element.38), channel_id=1, source_target_pairs={{1,0},{2,1},{3,2},{4,3},{5,4},{6,5},{7,6},{8,7},{9,8},{10,9},{11,1... | collective-permute-start | bytes 196616 | tf_op jit(solution)/shard_map/ppermute | solution.py:20
  505.9 10.6 %collective-permute-start.31 = (f32[1,64,256]{2,1,0:T(8,128)S(1)}, f32[1,64,256]{2,1,0:T(8,128)S(1)}, u32[]{:S(2)}, u32[]{:S(2)}) collective-permute-start(f32[1,64,256]{2,1,0:T(8,128)S(1)} %get-tuple-element.39), channel_id=1, source_target_pairs={{64,0},{128,64},{192,128},{65,1},{129,65},{193,129},{66,2},{130,66... | collective-permute-start | bytes 196616 | tf_op jit(solution)/shard_map/ppermute | solution.py:20
  507.2 10.6 %collective-permute-start.33 = (f32[1,64,256]{2,1,0:T(8,128)S(1)}, f32[1,64,256]{2,1,0:T(8,128)S(1)}, u32[]{:S(2)}, u32[]{:S(2)}) collective-permute-start(f32[1,64,256]{2,1,0:T(8,128)S(1)} %get-tuple-element.40), channel_id=1, source_target_pairs={{16,0},{32,16},{48,32},{17,1},{33,17},{49,33},{18,2},{34,18},{50,3... | collective-permute-start | bytes 196616 | tf_op jit(solution)/shard_map/ppermute | solution.py:20
  508.5 9.3 %collective-permute-start.34 = (f32[1,64,256]{2,1,0:T(8,128)S(1)}, f32[1,64,256]{2,1,0:T(8,128)S(1)}, u32[]{:S(2)}, u32[]{:S(2)}) collective-permute-start(f32[1,64,256]{2,1,0:T(8,128)S(1)} %get-tuple-element.41), channel_id=1, source_target_pairs={{0,1},{1,2},{2,3},{3,4},{4,5},{5,6},{6,7},{7,8},{8,9},{9,10},{10,1... | collective-permute-start | bytes 196616 | tf_op jit(solution)/shard_map/ppermute | solution.py:18
  512.2 5.6 collective-permute-start.32
  522.3 5.7 collective-permute-start.36
  528.0 6.1 collective-permute-start.37
  529.3 5.3 collective-permute-start.38
  534.7 6.3 collective-permute-start.39
  536.0 6.3 collective-permute-start.40
  542.2 6.2 collective-permute-start.41
  617.9 7.2 copy-start.5
  617.9 11.4 %copy-start.7 = (f32[64,6,256]{2,0,1:T(8,128)S(1)}, f32[64,6,256]{2,0,1:T(8,128)}, u32[]{:S(2)}) copy-start(f32[64,6,256]{2,0,1:T(8,128)} %copy-done.6) | copy-start | bytes 1179652
  621.3 8.0 %copy-start.12 = (f32[64,6,256]{2,0,1:T(8,128)S(1)}, f32[64,6,256]{2,0,1:T(8,128)}, u32[]{:S(2)}) copy-start(f32[64,6,256]{2,0,1:T(8,128)} %copy-done.11) | copy-start | bytes 1179652
  621.3 9.2 %copy-start.9 = (f32[64,6,256]{2,0,1:T(8,128)S(1)}, f32[64,6,256]{2,0,1:T(8,128)}, u32[]{:S(2)}) copy-start(f32[64,6,256]{2,0,1:T(8,128)} %copy-done.8) | copy-start | bytes 1179652
  626.4 13.7 %collective-permute-start.42 = (f32[1,64,256]{2,1,0:T(8,128)}, f32[1,64,256]{2,1,0:T(8,128)}, u32[]{:S(2)}, u32[]{:S(2)}) collective-permute-start(f32[1,64,256]{2,1,0:T(8,128)} %get-tuple-element.37), channel_id=1, source_target_pairs={{0,64},{64,128},{128,192},{1,65},{65,129},{129,193},{2,66},{66,130... | collective-permute-start | bytes 196616 | tf_op jit(solution)/shard_map/ppermute | solution.py:18
  629.4 19.1 %copy-start.22 = (f32[64]{0:T(128)S(1)}, f32[64]{0:T(128)}, u32[]{:S(2)}) copy-start(f32[64]{0:T(128)} %copy-done.21) | copy-start | bytes 772
  631.6 93.9 %copy-start.16 = (f32[1,1,1,64,1536]{4,3,2,1,0:T(8,128)S(1)}, f32[1,1,1,64,1536]{4,3,2,1,0:T(8,128)}, u32[]{:S(2)}) copy-start(f32[1,1,1,64,1536]{4,3,2,1,0:T(8,128)} %sub.78) | copy-start | bytes 1179652
  632.0 14.2 %collective-permute-start.47 = (f32[1,64,256]{2,1,0:T(8,128)S(1)}, f32[1,64,256]{2,1,0:T(8,128)S(1)}, u32[]{:S(2)}, u32[]{:S(2)}) collective-permute-start(f32[1,64,256]{2,1,0:T(8,128)S(1)} %get-tuple-element.32), channel_id=1, source_target_pairs={{1,0},{2,1},{3,2},{4,3},{5,4},{6,5},{7,6},{8,7},{9,8},{10,9},{11,1... | collective-permute-start | bytes 196616 | tf_op jit(solution)/shard_map/ppermute | solution.py:20
  633.9 11.4 %collective-permute-start.43 = (f32[1,64,256]{2,1,0:T(8,128)}, f32[1,64,256]{2,1,0:T(8,128)S(1)}, u32[]{:S(2)}, u32[]{:S(2)}) collective-permute-start(f32[1,64,256]{2,1,0:T(8,128)} %get-tuple-element.33), channel_id=1, source_target_pairs={{64,0},{128,64},{192,128},{65,1},{129,65},{193,129},{66,2},{130,66... | collective-permute-start | bytes 196616 | tf_op jit(solution)/shard_map/ppermute | solution.py:20
  635.2 10.9 %collective-permute-start.45 = (f32[1,64,256]{2,1,0:T(8,128)}, f32[1,64,256]{2,1,0:T(8,128)S(1)}, u32[]{:S(2)}, u32[]{:S(2)}) collective-permute-start(f32[1,64,256]{2,1,0:T(8,128)} %get-tuple-element.34), channel_id=1, source_target_pairs={{16,0},{32,16},{48,32},{17,1},{33,17},{49,33},{18,2},{34,18},{50,3... | collective-permute-start | bytes 196616 | tf_op jit(solution)/shard_map/ppermute | solution.py:20
  636.5 9.6 %collective-permute-start.46 = (f32[1,64,256]{2,1,0:T(8,128)}, f32[1,64,256]{2,1,0:T(8,128)S(1)}, u32[]{:S(2)}, u32[]{:S(2)}) collective-permute-start(f32[1,64,256]{2,1,0:T(8,128)} %get-tuple-element.35), channel_id=1, source_target_pairs={{0,1},{1,2},{2,3},{3,4},{4,5},{5,6},{6,7},{7,8},{8,9},{9,10},{10,1... | collective-permute-start | bytes 196616 | tf_op jit(solution)/shard_map/ppermute | solution.py:18
  640.1 5.9 collective-permute-start.44
  (10 other events, 33.8 us)
